TPU v7x, 128 devices: a whole 4x4x4 slice. The times are simulated.
128 devices in a mesh: dp: 2 (over x_lo), phase: 16 (over z, y), tensor: 4 (over x_hi, core).
Axes of the slice: x: 4 (x_hi: 2, x_lo: 2; x = x_hi * 2 + x_lo), y: 4, z: 4, core: 2. Of those that a mesh axis runs over, the one named last changes fastest.
Arguments:
- tokens: bfloat16 [2, 2048, 8192], P('dp', 'phase', 'tensor'), may hold values from -6 to 6
- bc_proj: bfloat16 [2, 2048, 2, 2048], P('dp', 'phase', None, 'tensor'), may hold values from -0.3984375 to 0.3984375
- step_sizes: bfloat16 [2, 256, 1024], P('dp', 'phase', 'tensor'), may hold values from 0.5 to 2
- decay_rates: float32 [128], P('tensor'), may hold values from 6.1035156e-05 to 0.02
- direct_weight: float32 [128], P('tensor'), may hold values from 0.5 to 1.5
- norm_gain: float32 [8192], P('tensor'), may hold values from 0.1 to 1.9
- routes: int32 [2, 256, 1], P('dp', 'phase'), may hold values from 0 to 1; in each aligned block of 16 rows (0 to 15, 16 to 31, ..., all dimensions but the last counted through in order) at most 16 rows name the same one
- segments: int32 [2, 4096], P('dp', 'phase'), may hold values from 0 to 3, never falling along the last dimension, each value on 1 to 2048 neighbouring positions
Outputs:
- mixed: bfloat16 [2, 2048, 8192], P('dp', 'phase', 'tensor')
Inputs may be any that keep to these rules, and one draw needn't show every extreme that they name: `routes`: no device sends more than 16 of its blocks to one data group. `segments`: document ids never fall along a row; each document covers 1 to 2048 positions, and one covers exactly 2048.
All inputs are finite; a program needn't handle non-finite values.
Results may differ from a plain program's by a relative error of at most 0.0075.
Values may be sent and summed in bfloat16 or wider, within the bound.
No kernel may reach another device: no remote copies, remote signals or barrier semaphores. Data moves between devices by JAX's collectives and lax.ppermute only.
A program may use at most 128 MiB of HBM per device.

v0:
```python
import jax
import jax.numpy as jnp
from jax import lax
from jax.sharding import PartitionSpec as P

HEAD_FEATURES = 64
STATE_ENTRIES = 256
LOCAL_HEADS = 128
BLOCK = 8


EPSILON = 1e-05
PRECISE = lax.Precision.HIGHEST


def prefix(shard, axis, join, neutral):
    place = lax.axis_index(axis)
    gathered = jax.tree.map(
        lambda a, kind: lax.all_gather(a.astype(kind), axis),
        shard,
        (jnp.bfloat16, jnp.bfloat16, jnp.bfloat16, jnp.bfloat16),
    )
    state = jax.tree.map(lambda a, e: jnp.zeros_like(a) + jnp.asarray(e, a.dtype), shard, neutral)

    def one(step, state):
        return join(
            state,
            jax.tree.map(
                lambda a, own: lax.dynamic_index_in_dim(a, step, 0, False).astype(own.dtype),
                gathered,
                shard,
            ),
        )

    return lax.fori_loop(0, place, one, state)


def stretch_pass(
    carry_state, prior_id, x_stretch, b_stretch, c_stretch, dt_stretch, doc_ids, decay_rates
):
    span_len = x_stretch.shape[0]
    head_count = x_stretch.shape[1]
    groups = b_stretch.shape[1]
    per_group = head_count // groups
    log_decay = jnp.cumsum(-decay_rates[:, None] * dt_stretch, axis=1)
    x_groups = x_stretch.astype(jnp.float32).reshape(span_len, groups, per_group, -1)
    b_float = b_stretch.astype(jnp.float32)
    last_id = doc_ids[-1]
    tail_decay = (
        jnp.where(doc_ids[None, :] == last_id, jnp.exp(log_decay[:, -1:] - log_decay), 0.0)
        * dt_stretch
    )
    scaled = x_groups * tail_decay.T.reshape(span_len, groups, per_group)[..., None]
    update = jnp.einsum("jgkp,jgn->gkpn", scaled, b_float, precision=PRECISE).reshape(
        carry_state.shape
    )
    through = jnp.where(prior_id == last_id, jnp.exp(log_decay[:, -1]), 0.0)
    new_state = through[:, None, None] * carry_state + update
    positions = jnp.arange(span_len)
    same_doc = (doc_ids[:, None] == doc_ids[None, :]) & (positions[:, None] >= positions[None, :])
    gaps = jnp.minimum(log_decay[:, :, None] - log_decay[:, None, :], 0.0)
    decay_mat = jnp.where(same_doc[None], jnp.exp(gaps), 0.0) * dt_stretch[:, None, :]
    scores = jnp.einsum("ign,jgn->gij", c_stretch, b_stretch, preferred_element_type=jnp.float32)
    weights = decay_mat.reshape(groups, per_group, span_len, span_len) * scores[:, None]
    inside = jnp.einsum("gkij,jgkp->igkp", weights, x_groups, precision=PRECISE)
    state_groups = carry_state.reshape(
        groups, per_group, carry_state.shape[1], carry_state.shape[2]
    )
    carried = jnp.einsum(
        "ign,gkpn->igkp", c_stretch.astype(jnp.float32), state_groups, precision=PRECISE
    )
    keep_in = jnp.where(doc_ids[None, :] == prior_id, jnp.exp(log_decay), 0.0)
    result = inside + keep_in.T.reshape(span_len, groups, per_group)[..., None] * carried
    return (new_state, last_id, result.reshape(span_len, head_count, -1))


def local_scan(x_stretches, b_stretches, c_stretches, dt_stretches, doc_stretches, decay_rates):
    head_count = x_stretches.shape[2]

    def advance(carry, pieces):
        new_state, last_id, result = stretch_pass(
            carry[0], carry[1], pieces[0], pieces[1], pieces[2], pieces[3], pieces[4], decay_rates
        )
        return ((new_state, last_id), result)

    start_carry = (
        jnp.zeros((head_count, HEAD_FEATURES, STATE_ENTRIES), jnp.float32),
        jnp.array(-1.0, jnp.float32),
    )
    final_carry, scan_results = lax.scan(
        advance, start_carry, (x_stretches, b_stretches, c_stretches, dt_stretches, doc_stretches)
    )
    return (final_carry[0], scan_results)


def join_pieces(earlier, later):
    decay_one, state_one, first_one, last_one = earlier
    decay_two, state_two, first_two, last_two = later
    joined = (first_two == last_one) | (last_one < 0) | (first_two < 0)
    factor = jnp.where(joined, decay_two, 0.0)
    joined_state = factor[:, None, None] * state_one + state_two
    joined_decay = jnp.where(joined, decay_one * decay_two, 0.0)
    joined_first = jnp.where(first_one < 0, first_two, first_one)
    joined_last = jnp.where(last_two < 0, last_one, last_two)
    return (joined_decay, joined_state, joined_first, joined_last)


def per_device(
    tokens, bc_proj, step_sizes, decay_rates, direct_weight, norm_gain, routes, segments
):
    feature_width = tokens.shape[2]
    tok_count = tokens.shape[1]
    heads_dev = decay_rates.shape[0]
    groups_dev = bc_proj.shape[3] // STATE_ENTRIES
    per_group = heads_dev // groups_dev
    blocks = tok_count // BLOCK
    n_groups = lax.axis_size("dp")
    capacity = max(2, 2 * blocks // n_groups)
    slots = n_groups * capacity
    section = slots * BLOCK
    span_len = min(128, section)
    block_count = section // span_len
    targets = routes[0, :, 0]
    positions = jnp.arange(blocks)
    earlier = positions[:, None] > positions[None, :]
    slot_rank = jnp.sum((targets[:, None] == targets[None, :]) & earlier, axis=1)
    slot_index = targets * capacity + slot_rank
    placing = (slot_index[:, None] == jnp.arange(slots)[None, :]).astype(jnp.bfloat16)
    x_send = jnp.einsum(
        "bs,bf->sf",
        placing,
        tokens.reshape(blocks, BLOCK * feature_width),
        preferred_element_type=jnp.float32,
    )
    x_send = x_send.astype(jnp.bfloat16).reshape(n_groups, capacity, BLOCK, feature_width)
    bc_send = jnp.einsum(
        "bs,bf->sf",
        placing,
        bc_proj.reshape(blocks, BLOCK * 2 * groups_dev * STATE_ENTRIES),
        preferred_element_type=jnp.float32,
    )
    bc_send = bc_send.astype(jnp.bfloat16).reshape(
        n_groups, capacity, BLOCK, 2, groups_dev, STATE_ENTRIES
    )
    dt_send = jnp.einsum("bs,bf->sf", placing, step_sizes[0], preferred_element_type=jnp.float32)
    dt_send = dt_send.astype(jnp.bfloat16).reshape(n_groups, capacity, heads_dev * BLOCK)
    x_got, bc_got, dt_got = (
        lax.all_to_all(x_send, "dp", split_axis=0, concat_axis=0, tiled=True),
        lax.all_to_all(bc_send, "dp", split_axis=0, concat_axis=0, tiled=True),
        lax.all_to_all(dt_send, "dp", split_axis=0, concat_axis=0, tiled=True),
    )
    x_stretches = x_got.reshape(block_count, span_len, heads_dev, HEAD_FEATURES)
    b_stretches = bc_got[:, :, :, 0].reshape(block_count, span_len, groups_dev, STATE_ENTRIES)
    c_section = bc_got[:, :, :, 1].reshape(section, groups_dev, STATE_ENTRIES)
    c_stretches = c_section.reshape(block_count, span_len, groups_dev, STATE_ENTRIES)
    dt_section = (
        dt_got.reshape(slots, heads_dev, BLOCK)
        .astype(jnp.float32)
        .transpose(1, 0, 2)
        .reshape(heads_dev, section)
    )
    dt_stretches = dt_section.reshape(heads_dev, block_count, span_len).transpose(1, 0, 2)
    doc_ids = segments[0].astype(jnp.float32)
    doc_stretches = doc_ids.reshape(block_count, span_len)
    log_decay = jnp.cumsum(-decay_rates[:, None] * dt_section, axis=1)
    through = jnp.where(doc_ids[0] == doc_ids[-1], jnp.exp(log_decay[:, -1]), 0.0)
    identity = (
        jnp.ones((heads_dev,), jnp.float32),
        jnp.zeros((heads_dev, HEAD_FEATURES, STATE_ENTRIES), jnp.float32),
        jnp.array(-1.0, jnp.float32),
        jnp.array(-1.0, jnp.float32),
    )
    end_state, local_out = local_scan(
        x_stretches, b_stretches, c_stretches, dt_stretches, doc_stretches, decay_rates
    )
    incoming = prefix((through, end_state, doc_ids[0], doc_ids[-1]), "phase", join_pieces, identity)
    in_state = incoming[1]
    in_last = incoming[3]
    keep_in = jnp.where(doc_ids[None, :] == in_last, jnp.exp(log_decay), 0.0)
    state_groups = in_state.reshape(groups_dev, per_group, HEAD_FEATURES, STATE_ENTRIES)
    carried = jnp.einsum(
        "ign,gkpn->igkp", c_section.astype(jnp.float32), state_groups, precision=PRECISE
    )
    carried = carried.reshape(section, heads_dev, HEAD_FEATURES)
    combined = (
        local_out.reshape(section, heads_dev, HEAD_FEATURES) + keep_in.T[:, :, None] * carried
    )
    combined = combined + direct_weight[None, :, None] * x_got.reshape(
        section, heads_dev, HEAD_FEATURES
    ).astype(jnp.float32)
    y_section = combined.astype(jnp.bfloat16).reshape(section, feature_width)
    returned_rows = lax.all_to_all(
        y_section.reshape(n_groups, capacity, BLOCK * feature_width),
        "dp",
        split_axis=0,
        concat_axis=0,
        tiled=True,
    )
    restored = jnp.einsum(
        "bs,sf->bf",
        placing,
        returned_rows.reshape(slots, BLOCK * feature_width),
        preferred_element_type=jnp.float32,
    )
    restored = restored.astype(jnp.bfloat16).reshape(tok_count, feature_width)
    values = restored.astype(jnp.float32)
    square_sums = lax.psum(jnp.sum(values * values, axis=1), "tensor")
    mixed = (
        values
        * lax.rsqrt(square_sums / (LOCAL_HEADS * HEAD_FEATURES) + EPSILON)[:, None]
        * norm_gain
    ).astype(jnp.bfloat16)
    return mixed.reshape(1, tok_count, feature_width)


def solution(mesh):
    return jax.shard_map(
        per_device,
        mesh=mesh,
        in_specs=(
            P("dp", "phase", "tensor"),
            P("dp", "phase", None, "tensor"),
            P("dp", "phase", "tensor"),
            P("tensor"),
            P("tensor"),
            P("tensor"),
            P("dp", "phase", None),
            P("dp", "phase"),
        ),
        out_specs=P("dp", "phase", "tensor"),
        check_vma=False,
    )
```

profile of v0, /device:TPU:120, one launch (start us, length us, event | category | flops | bytes accessed | tf_op | source)
XLA Modules:
  0.0 328.3 jit_solution(4840087548735297066)
XLA Ops:
  9.0 3.2 all-to-all-start
  16.1 3.5 %all-to-all-start.2 = ((bf16[2,16,8,2,2,256]{5,4,3,2,1,0:T(2,128)(2,1)}), bf16[2,16,8,2,2,256]{5,4,3,2,1,0:T(2,128)(2,1)S(1)}, u32[]{:S(2)}, u32[]{:S(2)}) async-start(bf16[2,16,8,2,2,256]{5,4,3,2,1,0:T(2,128)(2,1)} %reshape.294), calls=%async_computation.2 | async-start | bytes 1048576 | tf_op jit(solution)/shard_map/all_to_all | solution.py:149
  21.7 5.2 %all-to-all-done.2 = bf16[2,16,8,2,2,256]{5,4,3,2,1,0:T(2,128)(2,1)S(1)} async-done(((bf16[2,16,8,2,2,256]{5,4,3,2,1,0:T(2,128)(2,1)}), bf16[2,16,8,2,2,256]{5,4,3,2,1,0:T(2,128)(2,1)S(1)}, u32[]{:S(2)}, u32[]{:S(2)}) %all-to-all-start.2) | async-done | bytes 524320 | tf_op jit(solution)/shard_map/all_to_all | solution.py:149
  26.9 3.6 %all-to-all-start.1 = ((bf16[2,16,8,2048]{3,2,1,0:T(8,128)(2,1)}), bf16[2,16,8,2048]{3,2,1,0:T(8,128)(2,1)S(1)}, u32[]{:S(2)}, u32[]{:S(2)}) async-start(bf16[2,16,8,2048]{3,2,1,0:T(8,128)(2,1)} %bitcast.66), calls=%async_computation.1 | async-start | bytes 2097152 | tf_op jit(solution)/shard_map/all_to_all | solution.py:148
  31.6 11.0 %all-to-all-done.1 = bf16[2,16,8,2048]{3,2,1,0:T(8,128)(2,1)S(1)} async-done(((bf16[2,16,8,2048]{3,2,1,0:T(8,128)(2,1)}), bf16[2,16,8,2048]{3,2,1,0:T(8,128)(2,1)S(1)}, u32[]{:S(2)}, u32[]{:S(2)}) %all-to-all-start.1) | async-done | bytes 1048608 | tf_op jit(solution)/shard_map/all_to_all | solution.py:148
  43.7 3.2 reshape.292
  46.9 3.3 %copy.54 = bf16[2,128,32,64]{1,3,2,0:T(8,128)(2,1)S(1)} copy(bf16[2,128,32,64]{3,2,1,0:T(8,128)(2,1)} %reshape.292) | data formatting | bytes 2097152
  50.2 25.7 %while.33 = (s32[]{:T(128)}, f32[32,64,256]{2,1,0:T(8,128)}, f32[]{:T(128)}, f32[2,128,32,64]{1,3,2,0:T(8,128)}, f32[2,128]{1,0:T(2,128)S(1)}, /*index=5*/f32[32...) while((s32[]{:T(128)}, f32[32,64,256]{2,1,0:T(8,128)}, ...), condition=%wide.region_3.4_spmd.clone, body=%wide.region_1.3_spmd.clone.sunk | while | flops 2035876096 | bytes 46125748 | solution.py:90
  54.0 1.9 bitcast_add_fusion.2
  56.2 2.4 fusion.84
  66.0 3.5 %bitcast_add_fusion.2 = (f32[32,64,256]{2,1,0:T(8,128)}, f32[32,64,256]{2,1,0:T(8,128)S(1)}) fusion(f32[2,16,64,256]{3,2,1,0:T(8,128)S(1)} %fusion.81, f32[32]{0:T(128)S(1)} %broadcast_select_fusion.5, f32[32,64,256]{2,1,0:T(8,128)} %get-tuple-element.467, pred[]{:T(512)S(6)} %compare.3), kind=kLoop, calls=%fused_computation.3.clone.1 | loop fusion | flops 1572864 | bytes 8388737 | tf_op jit(solution)/shard_map/while/body/eval_jaxpr/add | solution.py:58
  69.8 2.4 fusion.84
  75.9 2.7 convert_element_type.146
  86.0 2.5 mul.184
  88.5 4.5 %mul.185 = f32[2,16,16384]{2,1,0:T(8,128)} reshape(f32[256,32,64]{2,1,0:T(8,128)} %mul.184) | data formatting | bytes 4194304 | tf_op jit(solution)/shard_map/mul | solution.py:188
  93.0 35.8 %all-reduce.3 = (bf16[16]{0:T(256)(128)(2,1)S(1)}, bf16[512]{0:T(512)(128)(2,1)S(1)}, bf16[16]{0:T(256)(128)(2,1)S(1)}) all-reduce(bf16[16]{0:T(256)(128)(2,1)S(1)} %dynamic-update-slice, bf16[512]{0:T(512)(128)(2,1)S(1)} %dynamic-update-slice.1, ...), channel_id=2, replica_groups=mesh['dp'=2,'phase'=16,'tensor'=4] {'phase'}, use_global_device_ids=true, to_apply=%add | all-reduce | flops 544 | bytes 2176 | tf_op jit(solution)/shard_map/all_gather | solution.py:19
  129.0 4.5 %copy.55 = f32[2,128,32,64]{3,2,1,0:T(8,128)} copy(f32[2,128,32,64]{1,3,2,0:T(8,128)S(1)} %copy-done.9) | data formatting | bytes 4194304 | tf_op jit(solution)/shard_map/while | solution.py:90
  133.5 4.1 %reshape.295 = f32[2,16,16384]{2,1,0:T(8,128)} reshape(f32[2,128,32,64]{3,2,1,0:T(8,128)} %copy.55) | data formatting | bytes 4194304 | tf_op jit(solution)/shard_map/reshape | solution.py:186
  139.2 50.2 %all-gather.6.cloned.1.call-done = bf16[512,64,256]{2,1,0:T(8,128)(2,1)} async-done(((bf16[32,64,256]{2,1,0:T(8,128)(2,1)}), bf16[512,64,256]{2,1,0:T(8,128)(2,1)}) %all-gather.6.cloned.1.call-update) | async-done | bytes 16777232 | tf_op jit(solution)/shard_map/all_gather | solution.py:19
  189.6 82.4 %while.32 = (s32[]{:T(128)}, f32[32,64,256]{2,1,0:T(8,128)S(1)}, f32[]{:T(128)}, s32[]{:T(128)}, bf16[16]{0:T(256)(128)(2,1)S(1)}, /*index=5*/bf16[16,32]{1,0:T(...) while((s32[]{:T(128)}, f32[32,64,256]{2,1,0:T(8,128)S(1)}, ...), condition=%wide.region_7.8_spmd, body=%wide.region_6.7_spmd.sunk | while | flops 1572940 | bytes 5243423 | solution.py:35
  202.5 1.6 convert_add_fusion.2
  208.0 1.6 convert_add_fusion.2
  213.5 1.6 convert_add_fusion.2
  235.5 1.6 convert_add_fusion.2
  272.0 2.4 convolution_bitcast_fusion.1
  274.4 5.5 %copy.60 = f32[256,2,16,64]{3,2,1,0:T(8,128)} copy(f32[256,2,16,64]{0,3,2,1:T(8,128)} %convolution_bitcast_fusion.1) | data formatting | bytes 4194304 | tf_op jit(solution)/shard_map/ign,gkpn->igkp/transpose | solution.py:181
  280.0 3.9 %reshape.298 = f32[2,16,16384]{2,1,0:T(8,128)} reshape(f32[256,2,16,64]{3,2,1,0:T(8,128)} %copy.60) | data formatting | bytes 4194304 | tf_op jit(solution)/shard_map/reshape | solution.py:184
  284.0 2.6 mul.181
  286.6 4.0 %mul.182 = f32[2,16,16384]{2,1,0:T(8,128)} reshape(f32[256,32,64]{2,1,0:T(8,128)} %mul.181) | data formatting | bytes 4194304 | tf_op jit(solution)/shard_map/mul | solution.py:186
  290.6 4.2 %add_convert_fusion = bf16[2,16,16384]{2,1,0:T(8,128)(2,1)S(1)} fusion(f32[2,16,16384]{2,1,0:T(8,128)S(1)} %copy-done.6, f32[2,16,16384]{2,1,0:T(8,128)} %reshape.304, f32[2,16,16384]{2,1,0:T(8,128)} %reshape.295, f32[2,16,16384]{2,1,0:T(8,128)} %mul.182, f32[2,16,16384]{2,1,0:T(8,128)} %reshape.298), kind=kLoop, calls=%fused_computation.56 | loop fusion | flops 2621440 | bytes 11534336 | tf_op jit(solution)/shard_map/convert_element_type | solution.py:191
  294.8 16.2 %all_to_all.20 = bf16[2,16,16384]{2,1,0:T(8,128)(2,1)S(1)} all-to-all(bf16[2,16,16384]{2,1,0:T(8,128)(2,1)S(1)} %add_convert_fusion), channel_id=1, replica_groups=mesh['dp'=2,'phase'=16,'tensor'=4] {'dp'}, dimensions={0} | all-to-all | bytes 2097152 | tf_op jit(solution)/shard_map/all_to_all | solution.py:192
  311.7 8.5 %psum.7 = f32[128]{0:T(128)S(1)} all-reduce(f32[128]{0:T(128)S(1)} %reduce_sum.19), channel_id=1, replica_groups=mesh['dp'=2,'phase'=16,'tensor'=4] {'tensor'}, use_global_device_ids=true, to_apply=%region_9.10 | all-reduce | flops 128 | bytes 1024 | tf_op jit(solution)/shard_map/psum | solution.py:207
  (179 shorter events, 67.3 us)
Async XLA Ops:
  6.5 1.6 copy-start
  6.5 8.4 %copy-start.12 = (bf16[1,128,2048]{2,1,0:T(8,128)(2,1)S(1)}, bf16[1,128,2048]{2,1,0:T(8,128)(2,1)}, u32[]{:S(2)}) copy-start(bf16[1,128,2048]{2,1,0:T(8,128)(2,1)} %param.12) | copy-start | bytes 1572868
  9.0 7.1 %all-to-all-start = ((bf16[2,16,256]{2,1,0:T(8,128)(2,1)}), bf16[2,16,256]{2,1,0:T(8,128)(2,1)S(1)}, u32[]{:S(2)}, u32[]{:S(2)}) async-start(bf16[2,16,256]{2,1,0:T(8,128)(2,1)} %bitcast.9), calls=%async_computation | async-start | bytes 32768 | tf_op jit(solution)/shard_map/all_to_all | solution.py:150
  16.1 10.9 %all-to-all-start.2 = ((bf16[2,16,8,2,2,256]{5,4,3,2,1,0:T(2,128)(2,1)}), bf16[2,16,8,2,2,256]{5,4,3,2,1,0:T(2,128)(2,1)S(1)}, u32[]{:S(2)}, u32[]{:S(2)}) async-start(bf16[2,16,8,2,2,256]{5,4,3,2,1,0:T(2,128)(2,1)} %reshape.294), calls=%async_computation.2 | async-start | bytes 1048576 | tf_op jit(solution)/shard_map/all_to_all | solution.py:149
  20.1 10.5 %copy-start.16 = (f32[32]{0:T(128)S(1)}, f32[32]{0:T(128)}, u32[]{:S(2)}) copy-start(f32[32]{0:T(128)} %param.15) | copy-start | bytes 388
  20.1 10.5 %copy-start.14 = (s32[1,256]{1,0:T(1,128)S(1)}, s32[1,256]{1,0:T(1,128)}, u32[]{:S(2)}) copy-start(s32[1,256]{1,0:T(1,128)} %param.19) | copy-start | bytes 3076
  26.9 15.7 %all-to-all-start.1 = ((bf16[2,16,8,2048]{3,2,1,0:T(8,128)(2,1)}), bf16[2,16,8,2048]{3,2,1,0:T(8,128)(2,1)S(1)}, u32[]{:S(2)}, u32[]{:S(2)}) async-start(bf16[2,16,8,2048]{3,2,1,0:T(8,128)(2,1)} %bitcast.66), calls=%async_computation.1 | async-start | bytes 2097152 | tf_op jit(solution)/shard_map/all_to_all | solution.py:148
  30.5 158.8 %all-gather.6.cloned.1.call-start = ((), (), s32[]{:S(2)}) async-start(), calls=%async_computation.4 | async-start | bytes 17825792 | tf_op jit(solution)/shard_map/all_gather | solution.py:19
  31.1 15.8 %copy-start.10 = (f32[32,32,8]{0,2,1:T(8,128)}, f32[32,32,8]{0,2,1:T(8,128)S(1)}, u32[]{:S(2)}) copy-start(f32[32,32,8]{0,2,1:T(8,128)S(1)} %copy.50) | copy-start | bytes 98308
  42.7 1.1 copy-start.4
  50.2 2.1 copy-start.2
  58.6 1.6 copy-start.7
  59.7 1.9 copy-start.3
  60.3 1.3 copy-start.8
  62.3 2.1 copy-start.2
  72.2 1.6 copy-start.7
  73.4 1.9 copy-start.3
  73.9 1.3 copy-start.8
  75.9 5.8 %copy-start.17 = (u32[128]{0:T(128)S(1)}, u32[128]{0:T(128)}, u32[]{:S(2)}) copy-start(u32[128]{0:T(128)} %constant.87) | copy-start | bytes 1540
  75.9 8.6 %copy-start.11 = (f32[32,32,8]{0,2,1:T(8,128)S(1)}, f32[32,32,8]{0,2,1:T(8,128)}, u32[]{:S(2)}) copy-start(f32[32,32,8]{0,2,1:T(8,128)} %copy-done.10) | copy-start | bytes 98308
  75.9 10.0 %copy-start.15 = (f32[32]{0:T(128)S(1)}, f32[32]{0:T(128)}, u32[]{:S(2)}) copy-start(f32[32]{0:T(128)} %param.16) | copy-start | bytes 388
  88.5 40.5 %copy-start.9 = (f32[2,128,32,64]{1,3,2,0:T(8,128)S(1)}, f32[2,128,32,64]{1,3,2,0:T(8,128)}, u32[]{:S(2)}) copy-start(f32[2,128,32,64]{1,3,2,0:T(8,128)} %get-tuple-element.192) | copy-start | bytes 6291460
  133.5 4.1 %copy-start.5 = (bf16[2,16,8,2048]{3,2,1,0:T(8,128)(2,1)S(1)}, bf16[2,16,8,2048]{3,2,1,0:T(8,128)(2,1)}, u32[]{:S(2)}) copy-start(bf16[2,16,8,2048]{3,2,1,0:T(8,128)(2,1)} %copy-done.4) | copy-start | bytes 3145732
  286.6 4.0 %copy-start.6 = (f32[2,16,16384]{2,1,0:T(8,128)S(1)}, f32[2,16,16384]{2,1,0:T(8,128)}, u32[]{:S(2)}) copy-start(f32[2,16,16384]{2,1,0:T(8,128)} %mul.185) | copy-start | bytes 6291460
  311.6 8.9 %copy-start.13 = (f32[2048]{0:T(1024)S(1)}, f32[2048]{0:T(1024)}, u32[]{:S(2)}) copy-start(f32[2048]{0:T(1024)} %param.17) | copy-start | bytes 24580
  311.6 9.9 %copy-start.1 = (bf16[1,16,256]{2,1,0:T(8,128)(2,1)S(1)}, bf16[1,16,256]{2,1,0:T(8,128)(2,1)}, u32[]{:S(2)}) copy-start(bf16[1,16,256]{2,1,0:T(8,128)(2,1)} %param.14) | copy-start | bytes 24580
Sparse Core Ops, SparseCore 0:
  78.8 110.4 all-gather.5
where the time goes:
time: 330 us; the launch traced here: 328 us
  local copies, waits for them, and re-layouts  73.4 us (22%)
  waiting for transfers between devices  67.3 us (20%)
  blocking collectives  60.5 us (18%)
  other arithmetic  43.3 us (13%)
  loops' own time  42.7 us (13%)
  between operations  16.7 us (5%)
  matrix products  13.9 us (4%)
  starting transfers between devices  10.3 us (3%)
    all_gather x1, waiting for transfers between devices, prefix(): lax.all_gather(a.astype(kind), axis)  50.2 us
    another operation x1, loops' own time, prefix(): return lax.fori_loop(0, place, one, state)  39.9 us
    all_gather x1, blocking collectives, prefix(): lax.all_gather(a.astype(kind), axis)  35.8 us
    add x15, other arithmetic, join_pieces(): joined_state = factor[:, None, None] * state_one + state_two  24.7 us
    dynamic_slice x30, local copies, waits for them, and re-layouts, one(): lax.dynamic_index_in_dim(a, step, 0, False).astype(own.dtype)  17.7 us
    all_to_all x1, blocking collectives, per_device(): lax.all_to_all(y_section.reshape(n_groups, capacity, BLOCK * feature_widt...  16.2 us
    all_to_all x1, waiting for transfers between devices, per_device(): lax.all_to_all(x_send, 'dp', split_axis=0, concat_axis=0, tiled=True)  11 us
    psum x1, blocking collectives, per_device(): square_sums = lax.psum(jnp.sum(values * values, axis=1), 'tensor')  8.54 us
  transfers between devices with their start and end apart: 4, of which 4 were waited for; matrix products, arithmetic and copies ran while one was open for 8% of the time, Pallas kernels for 0%

commit v1 on v0

v1 whole, which is shorter than its diff:
```python
import jax
import jax.numpy as jnp
from jax import lax
from jax.experimental import pallas as pl
from jax.experimental.pallas import tpu as pltpu
from jax.sharding import Mesh, PartitionSpec as P

EPSILON = 1e-05
F32 = jnp.float32
BF16 = jnp.bfloat16
HIGH = lax.Precision.HIGHEST
TOK = 128
PEERS = 8
SPAN = TOK * PEERS
WIDE = 256
AUX = 8


def dot(a, b, dims, precision=None):
    return lax.dot_general(a, b, (dims, ((), ())), precision=precision, preferred_element_type=F32)


def iota(shape, dim):
    return lax.broadcasted_iota(jnp.int32, shape, dim)


def ones_where(cond, dtype=F32):
    return jnp.where(cond, 1.0, 0.0).astype(dtype)


def pack_kernel(where_ref, tok_ref, b_ref, c_ref, dt_ref, route_ref, seg_ref, out_ref):
    block_of = ones_where(iota((16, TOK), 1) // 8 == iota((16, TOK), 0), BF16)
    spread = dot(dt_ref[...], block_of, ((0,), (0,)))
    same_u = iota((256, TOK), 0) % 8 == iota((256, TOK), 1) % 8
    spread = jnp.where(same_u, spread, 0.0).astype(BF16)
    head_of = ones_where(iota((32, 256), 1) // 8 == iota((32, 256), 0), BF16)
    dt_rows = dot(head_of, spread, ((1,), (0,)))
    route = jnp.broadcast_to(route_ref[...].astype(F32), (16, TOK)).astype(BF16)
    route_row = dot(route, block_of, ((0,), (0,)))
    route_col = dot(block_of, route, ((0,), (0,)))
    ahead = (route_row == route_col) & (iota((TOK, TOK), 0) < iota((TOK, TOK), 1))
    place = jnp.sum(ones_where(ahead), axis=0, keepdims=True) + (where_ref[0] * TOK).astype(F32)
    segs = seg_ref[...]
    lane = iota((1, TOK), 1)
    starts = jnp.zeros((1, TOK), F32)
    for k in range(3):
        starts = jnp.where(lane == k, jnp.sum(ones_where(segs < k + 1), axis=1, keepdims=True), starts)
    row = iota((AUX, TOK), 0)
    for o in range(PEERS):
        g = o // 4
        out_ref[o, :TOK, 0:WIDE] = tok_ref[:, o * WIDE : (o + 1) * WIDE]
        out_ref[o, :TOK, WIDE : 2 * WIDE] = b_ref[:, g * WIDE : (g + 1) * WIDE]
        out_ref[o, :TOK, 2 * WIDE : 3 * WIDE] = c_ref[:, g * WIDE : (g + 1) * WIDE]
        aux = jnp.where(row == 4, route_row[0:1], jnp.where(row == 5, place, starts))
        for h in range(4):
            aux = jnp.where(row == h, dt_rows[o * 4 + h : o * 4 + h + 1], aux)
        out_ref[o, TOK : TOK + AUX, :] = jnp.concatenate([aux.astype(BF16)] * 6, axis=1)


def rate_lanes(where_ref, ref):
    lane = iota((1, WIDE), 1) // 64
    first = where_ref[1] * 4
    out = jnp.full((1, WIDE), ref[first], F32)
    for h in range(1, 4):
        out = jnp.where(lane == h, ref[first + h], out)
    return out


def state_kernel(where_ref, rate_ref, r_ref, e_ref, f_ref, xs_ref, m_ref, fm_ref, meta_ref, dt_ref, bm_ref):
    rate = rate_lanes(where_ref, rate_ref)
    spread = ones_where(iota((AUX, WIDE), 1) // 64 == iota((AUX, WIDE), 0), BF16)
    pick_route = ones_where(iota((AUX, TOK), 0) == 4, BF16)
    pick_place = ones_where(iota((AUX, TOK), 0) == 5, BF16)
    starts = [[None] * 3, [None] * 3]
    rows, cols = [], []
    for q in range(PEERS):
        y, j = q // 2, q % 2
        aux = r_ref[j * 4 + y, TOK : TOK + AUX, 0:TOK]
        auxf = aux.astype(F32)
        dt_ref[q * TOK : (q + 1) * TOK, :] = dot(aux, spread, ((0,), (0,))).astype(BF16)
        rows.append((auxf[4:5], auxf[5:6] + y * 256.0))
        cols.append((dot(aux, pick_route, ((0,), (0,))), dot(aux, pick_place, ((0,), (0,))) + y * 256.0))
        for k in range(3):
            n = auxf[6:7, k : k + 1]
            starts[j][k] = n if starts[j][k] is None else starts[j][k] + n

    def key_of(route, place):
        second = route > 0.5
        doc = 4.0 * route
        for k in range(3):
            doc = doc + ones_where(place >= jnp.where(second, starts[1][k], starts[0][k]))
        return doc

    key_rows = [key_of(*p) for p in rows]
    key_cols = [key_of(*p) for p in cols]
    first, last = [], []
    for d in range(2):
        first.append(sum(ones_where(starts[d][k] <= 0.0) for k in range(3)))
        last.append(sum(ones_where(starts[d][k] <= SPAN - 1.0) for k in range(3)))
    causal = iota((TOK, TOK), 0) >= iota((TOK, TOK), 1)
    for i in range(PEERS):
        for jj in range(i + 1 + (i + 1) % 2):
            if jj > i:
                m = jnp.zeros((TOK, TOK), BF16)
            else:
                same = key_cols[i] == key_rows[jj]
                m = ones_where(same & causal if i == jj else same, BF16)
            m_ref[i * TOK : (i + 1) * TOK, jj * TOK : (jj + 1) * TOK] = m
        for d in range(2):
            fm_ref[i * TOK : (i + 1) * TOK, d * TOK : (d + 1) * TOK] = ones_where(
                key_cols[i] == first[d] + 4.0 * d, BF16
            )
            lm = ones_where(key_cols[i] == last[d] + 4.0 * d, BF16)
            src = (i % 2) * 4 + i // 2
            for half in range(2):
                bm_ref[d, i * TOK : (i + 1) * TOK, half * TOK : (half + 1) * TOK] = (
                    r_ref[src, :TOK, WIDE + half * TOK : WIDE + (half + 1) * TOK] * lm
                )
    for b in range(4):
        sl = slice(b * 256, (b + 1) * 256)
        total = dot(m_ref[sl, : (b + 1) * 256], dt_ref[: (b + 1) * 256, :], ((1,), (0,)))
        f_ref[sl, :] = jnp.exp(-rate * total)
        grow = jnp.exp(rate * total) * dt_ref[sl, :].astype(F32)
        for s in range(2):
            x = r_ref[s * 4 + b, :TOK, 0:WIDE].astype(F32)
            at = b * 256 + s * TOK
            xs_ref[at : at + TOK, :] = (x * grow[s * TOK : (s + 1) * TOK]).astype(BF16)
    row8 = iota((AUX, WIDE), 0)
    for d in range(2):
        total = jnp.zeros((AUX, WIDE), F32)
        for q in range(PEERS):
            lm = jnp.broadcast_to(ones_where(key_rows[q] == last[d] + 4.0 * d), (AUX, TOK)).astype(BF16)
            total = total + dot(lm, dt_ref[q * TOK : (q + 1) * TOK, :], ((1,), (0,)))
        through = jnp.exp(-rate * total)
        e = dot(bm_ref[d], xs_ref[...], ((0,), (0,))) * through[0:1]
        e_ref[d, 0:WIDE, :] = e.astype(BF16)
        e_ref[d, WIDE : WIDE + AUX, :] = jnp.where(row8 == 0, through, last[d]).astype(BF16)
    meta_ref[...] = jnp.where(iota((AUX, TOK), 0) == 0, first[0], first[1])


def inside_kernel(where_ref, weight_ref, r_ref, f_ref, xs_ref, m_ref, fm_ref, base_ref, cm_ref, b_ref, c_ref):
    weight = rate_lanes(where_ref, weight_ref)
    for q in range(PEERS):
        src = (q % 2) * 4 + q // 2
        sl = slice(q * TOK, (q + 1) * TOK)
        b_ref[sl, :] = r_ref[src, :TOK, WIDE : 2 * WIDE]
        c = r_ref[src, :TOK, 2 * WIDE : 3 * WIDE]
        c_ref[sl, :] = c
        for d in range(2):
            fm = fm_ref[sl, d * TOK : (d + 1) * TOK]
            for half in range(2):
                at = d * WIDE + half * TOK
                cm_ref[sl, at : at + TOK] = c[:, half * TOK : (half + 1) * TOK] * fm
    for i in range(4):
        si = slice(i * 256, (i + 1) * 256)
        acc = jnp.zeros((256, WIDE), F32)
        for j in range(i + 1):
            sj = slice(j * 256, (j + 1) * 256)
            s = dot(c_ref[si, :], b_ref[sj, :], ((1,), (1,)))
            w = (s * m_ref[si, sj].astype(F32)).astype(BF16)
            acc = acc + dot(w, xs_ref[sj, :], ((1,), (0,)))
        acc = acc * f_ref[si, :]
        for s in range(2):
            x = r_ref[s * 4 + i, :TOK, 0:WIDE].astype(F32)
            at = i * 256 + s * TOK
            base_ref[at : at + TOK, :] = acc[s * TOK : (s + 1) * TOK] + weight * x


def carry_kernel(base_ref, f_ref, cm_ref, e1_ref, e2_ref, meta_ref, y_ref, h_ref):
    for d in range(2):
        first = meta_ref[d : d + 1, 0:1]
        joined1 = e1_ref[d, WIDE + 1 : WIDE + 2, :].astype(F32) == first
        joined2 = joined1 & (e2_ref[d, WIDE + 1 : WIDE + 2, :].astype(F32) == first)
        through = jnp.where(joined2, e1_ref[d, WIDE : WIDE + 1, :].astype(F32), 0.0)
        near = jnp.where(joined1, e1_ref[d, 0:WIDE, :].astype(F32), 0.0)
        h_ref[d * WIDE : (d + 1) * WIDE, :] = (near + through * e2_ref[d, 0:WIDE, :].astype(F32)).astype(BF16)
    for q in range(PEERS):
        sl = slice(q * TOK, (q + 1) * TOK)
        y = base_ref[sl, :] + f_ref[sl, :] * dot(cm_ref[sl, :], h_ref[...], ((1,), (0,)))
        y_ref[(q % 2) * 4 + q // 2] = y.astype(BF16)


def square_kernel(y_ref, s_ref):
    acc = jnp.zeros((TOK, WIDE), F32)
    for o in range(PEERS):
        v = y_ref[o].astype(F32)
        acc = acc + v * v
    s_ref[...] = dot(jnp.ones((AUX, WIDE), F32), acc, ((1,), (1,)), HIGH)


def scale_kernel(y_ref, s0_ref, s1_ref, s2_ref, s3_ref, gain_ref, out_ref, *, features):
    total = (s0_ref[...] + s1_ref[...]) + (s2_ref[...] + s3_ref[...])
    pick = ones_where(iota((AUX, TOK), 0) == 0)
    col = dot(total, pick, ((0,), (0,)), HIGH)
    scale = lax.rsqrt(col / features + EPSILON)
    scale = jnp.concatenate([scale, scale], axis=1)
    for o in range(PEERS):
        sl = slice(o * WIDE, (o + 1) * WIDE)
        out_ref[:, sl] = (y_ref[o].astype(F32) * scale * gain_ref[:, sl]).astype(BF16)


VM = pl.BlockSpec(memory_space=pltpu.VMEM)
SM = pl.BlockSpec(memory_space=pltpu.SMEM)


def call(kernel, specs, outs, *args, scratch=()):
    out_shape = [jax.ShapeDtypeStruct(s, d) for s, d in outs]
    return pl.pallas_call(
        kernel,
        in_specs=specs,
        out_specs=[VM] * len(outs),
        out_shape=out_shape,
        scratch_shapes=list(scratch),
        name=kernel.__name__ if hasattr(kernel, "__name__") else "scale_kernel",
    )(*args)


def per_device(tokens, bc_proj, step_sizes, decay_rates, direct_weight, norm_gain, routes, segments):
    j = lax.axis_index("dp")
    y = lax.axis_index("y")
    where = jnp.stack([j, j * 4 + y]).astype(jnp.int32)
    b, c = bc_proj[0, :, 0], bc_proj[0, :, 1]
    (send,) = call(
        pack_kernel,
        [SM, VM, VM, VM, VM, VM, VM],
        [((PEERS, TOK + AUX, 3 * WIDE), BF16)],
        where, tokens[0], b, c, step_sizes[0], routes[0], segments,
    )
    got = lax.all_to_all(send, ("dp", "y"), split_axis=0, concat_axis=0, tiled=True)
    e, f, xs, m, fm, meta = call(
        state_kernel,
        [SM, SM, VM],
        [
            ((2, WIDE + AUX, WIDE), BF16),
            ((SPAN, WIDE), F32),
            ((SPAN, WIDE), BF16),
            ((SPAN, SPAN), BF16),
            ((SPAN, 2 * TOK), BF16),
            ((AUX, TOK), F32),
        ],
        where, decay_rates, got,
        scratch=[pltpu.VMEM((SPAN, WIDE), BF16), pltpu.VMEM((2, SPAN, WIDE), BF16)],
    )
    e1 = lax.ppermute(e, "z", [(i, i + 1) for i in range(3)])
    e2 = lax.ppermute(e, "z", [(i, i + 2) for i in range(2)])
    base, cm = call(
        inside_kernel,
        [SM, SM, VM, VM, VM, VM, VM],
        [((SPAN, WIDE), F32), ((SPAN, 2 * WIDE), BF16)],
        where, direct_weight, got, f, xs, m, fm,
        scratch=[pltpu.VMEM((SPAN, WIDE), BF16), pltpu.VMEM((SPAN, WIDE), BF16)],
    )
    (out,) = call(
        carry_kernel,
        [VM] * 6,
        [((PEERS, TOK, WIDE), BF16)],
        base, f, cm, e1, e2, meta,
        scratch=[pltpu.VMEM((2 * WIDE, WIDE), BF16)],
    )
    back = lax.all_to_all(out, ("dp", "y"), split_axis=0, concat_axis=0, tiled=True)
    (s0,) = call(square_kernel, [VM], [((AUX, TOK), F32)], back)
    others = [lax.ppermute(s0, "tensor", [(i, (i + k) % 4) for i in range(4)]) for k in (1, 2, 3)]

    def scale(*refs):
        scale_kernel(*refs, features=128 * 64)

    (mixed,) = call(scale, [VM] * 6, [((TOK, PEERS * WIDE), BF16)], back, s0, *others, norm_gain[None])
    return mixed[None]


def solution(mesh):
    fine = Mesh(mesh.devices.reshape(2, 4, 4, 4), ("dp", "z", "y", "tensor"))
    rows = ("z", "y")
    return jax.shard_map(
        per_device,
        mesh=fine,
        in_specs=(
            P("dp", rows, "tensor"),
            P("dp", rows, None, "tensor"),
            P("dp", rows, "tensor"),
            P("tensor"),
            P("tensor"),
            P("tensor"),
            P("dp", rows, None),
            P("dp", rows),
        ),
        out_specs=P("dp", rows, "tensor"),
        check_vma=False,
    )
```

time: 330 us -> 86.9 us (0.26)
  the two profiles are of different devices: /device:TPU:120 before, /device:TPU:64 now
where the time goes in v1:
time: 86.9 us; the launch traced here: 86.5 us
  blocking collectives  42.2 us (49%)
  Pallas kernels  20.1 us (23%)
  waiting for transfers between devices  10.9 us (13%)
  starting transfers between devices  7.76 us (9%)
  local copies, waits for them, and re-layouts  4.84 us (6%)
    all_to_all x1, blocking collectives, per_device(): lax.all_to_all(send, ('dp', 'y'), split_axis=0, concat_axis=0, tiled=True)  28.1 us
    pallas_call x6, Pallas kernels, call(): pl.pallas_call(kernel, in_specs=specs, out_specs=[VM] * len(outs), out_sh...  20.1 us
    all_to_all x1, blocking collectives, per_device(): lax.all_to_all(out, ('dp', 'y'), split_axis=0, concat_axis=0, tiled=True)  14.1 us
    ppermute x3, waiting for transfers between devices, per_device(): lax.ppermute(s0, 'tensor', [(i, (i + k) % 4) for i in range(4)])  4.51 us
    ppermute x1, starting transfers between devices, per_device(): e1 = lax.ppermute(e, 'z', [(i, i + 1) for i in range(3)])  3.53 us
    ppermute x1, waiting for transfers between devices, per_device(): e2 = lax.ppermute(e, 'z', [(i, i + 2) for i in range(2)])  3.44 us
    ppermute x1, waiting for transfers between devices, per_device(): e1 = lax.ppermute(e, 'z', [(i, i + 1) for i in range(3)])  2.97 us
    ppermute x3, starting transfers between devices, per_device(): lax.ppermute(s0, 'tensor', [(i, (i + k) % 4) for i in range(4)])  2.95 us
  transfers between devices with their start and end apart: 5, of which 4 were waited for; matrix products, arithmetic and copies ran while one was open for 0% of the time, Pallas kernels for 5%

profile of v1, /device:TPU:64, one launch (start us, length us, event | category | flops | bytes accessed | tf_op | source)
XLA Modules:
  0.0 86.5 jit_solution(17304307936425105207)
XLA Ops:
  0.0 1.3 %copy.11.route_ref = s32[16,1]{1,0:T(8,128)} copy(s32[16,1]{0,1:T(1,128)} %bitcast.14) | data formatting | bytes 128 | tf_op jit(solution)/shard_map/squeeze | solution.py:227
  1.3 1.5 %fusion = (bf16[1,128,1,512]{3,2,1,0:T(2,128)(2,1)S(1)}, bf16[1,128,1,512]{3,2,1,0:T(2,128)(2,1)S(1)}) fusion(bf16[1,128,2,512]{3,2,1,0:T(2,128)(2,1)} %param.9), kind=kLoop, calls=%fused_computation.3 | loop fusion | bytes 524288 | tf_op jit(solution)/shard_map/slice | solution.py:222
  2.8 0.7 pad_add_fusion.where_ref
  3.5 0.7 copy_bitcast_fusion
  4.2 2.8 %pack_kernel.1 = bf16[8,136,768]{2,1,0:T(8,128)(2,1)} custom-call(s32[2]{0:T(128)} %pad_add_fusion.where_ref, bf16[128,2048]{1,0:T(8,128)(2,1)} %bitcast.11, bf16[128,512]{1,0:T(8,128)(2,1)} %get-tuple-element.24.b_ref, bf16[128,512]{1,0:T(8,128)(2,1)} %get-tuple-element.23.c_ref, bf16[16,256]{1,0:T(8,128)(2,1)} %bitcast.12, s32[16,1]{1,0:T(8,128)} %copy.11.route_ref, ...), custom_call_target="tpu_custom_call" | custom-call | tf_op jit(solution)/shard_map/pack_kernel/pallas_call | solution.py:208
  7.0 28.1 %all_to_all.10.r_ref = bf16[8,136,768]{2,1,0:T(8,128)(2,1)} all-to-all(bf16[8,136,768]{2,1,0:T(8,128)(2,1)} %pack_kernel.1), channel_id=1, replica_groups=mesh['dp'=2,'z'=4,'y'=4,'tensor'=4] {'dp','y'}, dimensions={0} | all-to-all | bytes 3342336 | tf_op jit(solution)/shard_map/all_to_all | solution.py:229
  35.1 5.2 %state_kernel.1 = (bf16[2,264,256]{2,1,0:T(8,128)(2,1)}, f32[1024,256]{1,0:T(8,128)}, bf16[1024,256]{1,0:T(8,128)(2,1)}, bf16[1024,1024]{1,0:T(8,128)(2,1)}, bf1...) custom-call(s32[2]{0:T(128)} %pad_add_fusion.where_ref, f32[32]{0:T(128)} %rate_ref.1, bf16[8,136,768]{2,1,0:T(8,128)(2,1)} %all_to_all.10.r_ref), custom_call_target="tpu_custom_call" | custom-call | tf_op jit(solution)/shard_map/state_kernel/pallas_call | solution.py:208
  40.3 1.3 %collective-permute-start.1 = (bf16[2,264,256]{2,1,0:T(8,128)(2,1)}, bf16[2,264,256]{2,1,0:T(8,128)(2,1)S(1)}, u32[]{:S(2)}, u32[]{:S(2)}) collective-permute-start(bf16[2,264,256]{2,1,0:T(8,128)(2,1)} %get-tuple-element.19), channel_id=1, source_target_pairs={{0,32},{16,48},{1,33},{17,49},{2,34},{18,50},{3,35},{19,51},{4,36}... | collective-permute-start | bytes 811016 | tf_op jit(solution)/shard_map/ppermute | solution.py:245
  41.5 3.5 %collective-permute-start = (bf16[2,264,256]{2,1,0:T(8,128)(2,1)}, bf16[2,264,256]{2,1,0:T(8,128)(2,1)S(1)}, u32[]{:S(2)}, u32[]{:S(2)}) collective-permute-start(bf16[2,264,256]{2,1,0:T(8,128)(2,1)} %get-tuple-element.19), channel_id=1, source_target_pairs={{0,16},{16,32},{32,48},{1,17},{17,33},{33,49},{2,18},{18,34},{34,5... | collective-permute-start | bytes 811016 | tf_op jit(solution)/shard_map/ppermute | solution.py:244
  45.1 4.7 %inside_kernel.1 = (f32[1024,256]{1,0:T(8,128)}, bf16[1024,512]{1,0:T(8,128)(2,1)}) custom-call(s32[2]{0:T(128)} %pad_add_fusion.where_ref, f32[32]{0:T(128)} %weight_ref.1, bf16[8,136,768]{2,1,0:T(8,128)(2,1)} %all_to_all.10.r_ref, f32[1024,256]{1,0:T(8,128)} %get-tuple-element.13.f_ref, bf16[1024,256]{1,0:T(8,128)(2,1)} %get-tuple-element.14.xs_ref, ...), custom_call_target="tpu_custom_call" | custom-call | tf_op jit(solution)/shard_map/inside_kernel/pallas_call | solution.py:208
  49.8 3.4 %collective-permute-done.1.e2_ref = bf16[2,264,256]{2,1,0:T(8,128)(2,1)S(1)} collective-permute-done((bf16[2,264,256]{2,1,0:T(8,128)(2,1)}, bf16[2,264,256]{2,1,0:T(8,128)(2,1)S(1)}, u32[]{:S(2)}, u32[]{:S(2)}) %collective-permute-start.1) | collective-permute-done | bytes 270368 | tf_op jit(solution)/shard_map/ppermute | solution.py:245
  53.2 0.0 copy-start
  53.2 3.0 %collective-permute-done.e1_ref = bf16[2,264,256]{2,1,0:T(8,128)(2,1)S(1)} collective-permute-done((bf16[2,264,256]{2,1,0:T(8,128)(2,1)}, bf16[2,264,256]{2,1,0:T(8,128)(2,1)S(1)}, u32[]{:S(2)}, u32[]{:S(2)}) %collective-permute-start) | collective-permute-done | bytes 270368 | tf_op jit(solution)/shard_map/ppermute | solution.py:244
  56.2 0.0 copy-start.1
  56.2 0.0 copy-done
  56.2 0.7 copy-done.1
  56.9 3.3 %carry_kernel.1 = bf16[8,128,256]{2,1,0:T(8,128)(2,1)} custom-call(f32[1024,256]{1,0:T(8,128)} %get-tuple-element.17.base_ref, f32[1024,256]{1,0:T(8,128)} %get-tuple-element.13.f_ref, bf16[1024,512]{1,0:T(8,128)(2,1)} %get-tuple-element.18.cm_ref, bf16[2,264,256]{2,1,0:T(8,128)(2,1)} %copy-done.1, bf16[2,264,256]{2,1,0:T(8,128)(2,1)} %copy-done, ...), custom_call_target="tpu_custom_call" | custom-call | tf_op jit(solution)/shard_map/carry_kernel/pallas_call | solution.py:208
  60.2 14.1 %all_to_all.11.y_ref.refs_0_ = bf16[8,128,256]{2,1,0:T(8,128)(2,1)} all-to-all(bf16[8,128,256]{2,1,0:T(8,128)(2,1)} %carry_kernel.1), channel_id=1, replica_groups=mesh['dp'=2,'z'=4,'y'=4,'tensor'=4] {'dp','y'}, dimensions={0} | all-to-all | bytes 1048576 | tf_op jit(solution)/shard_map/all_to_all | solution.py:260
  74.3 1.9 %square_kernel.1.refs_1_ = f32[8,128]{1,0:T(8,128)} custom-call(bf16[8,128,256]{2,1,0:T(8,128)(2,1)} %all_to_all.11.y_ref.refs_0_), custom_call_target="tpu_custom_call" | custom-call | tf_op jit(solution)/shard_map/square_kernel/pallas_call | solution.py:208
  76.2 0.3 collective-permute-start.4
  76.5 2.4 %collective-permute-start.3 = (f32[8,128]{1,0:T(8,128)}, f32[8,128]{1,0:T(8,128)S(1)}, u32[]{:S(2)}, u32[]{:S(2)}) collective-permute-start(f32[8,128]{1,0:T(8,128)} %square_kernel.1.refs_1_), channel_id=1, source_target_pairs={{0,2},{1,3},{2,0},{3,1},{4,6},{5,7},{6,4},{7,5},{8,10},{9,11},{10,... | collective-permute-start | bytes 12296 | tf_op jit(solution)/shard_map/ppermute | solution.py:262
  78.9 0.2 collective-permute-start.2
  79.2 0.0 collective-permute-done.4.refs_4_
  79.2 0.0 copy-start.2
  79.2 2.7 %collective-permute-done.3.refs_3_ = f32[8,128]{1,0:T(8,128)S(1)} collective-permute-done((f32[8,128]{1,0:T(8,128)}, f32[8,128]{1,0:T(8,128)S(1)}, u32[]{:S(2)}, u32[]{:S(2)}) %collective-permute-start.3) | collective-permute-done | bytes 4128 | tf_op jit(solution)/shard_map/ppermute | solution.py:262
  81.8 0.0 copy-start.3
  81.8 1.8 %collective-permute-done.2.refs_2_ = f32[8,128]{1,0:T(8,128)S(1)} collective-permute-done((f32[8,128]{1,0:T(8,128)}, f32[8,128]{1,0:T(8,128)S(1)}, u32[]{:S(2)}, u32[]{:S(2)}) %collective-permute-start.2) | collective-permute-done | bytes 4128 | tf_op jit(solution)/shard_map/ppermute | solution.py:262
  83.7 0.0 copy-start.4
  83.7 0.0 copy-done.2
  83.7 0.0 copy-done.3
  83.7 0.6 copy-done.4
  84.3 2.2 %scale.1 = bf16[128,2048]{1,0:T(8,128)(2,1)} custom-call(bf16[8,128,256]{2,1,0:T(8,128)(2,1)} %all_to_all.11.y_ref.refs_0_, f32[8,128]{1,0:T(8,128)} %square_kernel.1.refs_1_, f32[8,128]{1,0:T(8,128)} %copy-done.4, f32[8,128]{1,0:T(8,128)} %copy-done.3, f32[8,128]{1,0:T(8,128)} %copy-done.2, f32[1,2048]{1,0:T(1,128)} %bitcast.13), custom_call_target="tpu_custom_call" | custom-call | tf_op jit(solution)/shard_map/scale/pallas_call | solution.py:208
Async XLA Ops:
  40.3 13.0 %collective-permute-start.1 = (bf16[2,264,256]{2,1,0:T(8,128)(2,1)}, bf16[2,264,256]{2,1,0:T(8,128)(2,1)S(1)}, u32[]{:S(2)}, u32[]{:S(2)}) collective-permute-start(bf16[2,264,256]{2,1,0:T(8,128)(2,1)} %get-tuple-element.19), channel_id=1, source_target_pairs={{0,32},{16,48},{1,33},{17,49},{2,34},{18,50},{3,35},{19,51},{4,36}... | collective-permute-start | bytes 811016 | tf_op jit(solution)/shard_map/ppermute | solution.py:245
  41.5 14.6 %collective-permute-start = (bf16[2,264,256]{2,1,0:T(8,128)(2,1)}, bf16[2,264,256]{2,1,0:T(8,128)(2,1)S(1)}, u32[]{:S(2)}, u32[]{:S(2)}) collective-permute-start(bf16[2,264,256]{2,1,0:T(8,128)(2,1)} %get-tuple-element.19), channel_id=1, source_target_pairs={{0,16},{16,32},{32,48},{1,17},{17,33},{33,49},{2,18},{18,34},{34,5... | collective-permute-start | bytes 811016 | tf_op jit(solution)/shard_map/ppermute | solution.py:244
  53.2 3.0 %copy-start = (bf16[2,264,256]{2,1,0:T(8,128)(2,1)}, bf16[2,264,256]{2,1,0:T(8,128)(2,1)S(1)}, u32[]{:S(2)}) copy-start(bf16[2,264,256]{2,1,0:T(8,128)(2,1)S(1)} %collective-permute-done.1.e2_ref) | copy-start | bytes 811012
  56.2 0.7 copy-start.1
  76.2 3.0 %collective-permute-start.4 = (f32[8,128]{1,0:T(8,128)}, f32[8,128]{1,0:T(8,128)S(1)}, u32[]{:S(2)}, u32[]{:S(2)}) collective-permute-start(f32[8,128]{1,0:T(8,128)} %square_kernel.1.refs_1_), channel_id=1, source_target_pairs={{0,3},{1,0},{2,1},{3,2},{4,7},{5,4},{6,5},{7,6},{8,11},{9,8},{10,9... | collective-permute-start | bytes 12296 | tf_op jit(solution)/shard_map/ppermute | solution.py:262
  76.5 5.3 %collective-permute-start.3 = (f32[8,128]{1,0:T(8,128)}, f32[8,128]{1,0:T(8,128)S(1)}, u32[]{:S(2)}, u32[]{:S(2)}) collective-permute-start(f32[8,128]{1,0:T(8,128)} %square_kernel.1.refs_1_), channel_id=1, source_target_pairs={{0,2},{1,3},{2,0},{3,1},{4,6},{5,7},{6,4},{7,5},{8,10},{9,11},{10,... | collective-permute-start | bytes 12296 | tf_op jit(solution)/shard_map/ppermute | solution.py:262
  78.9 4.7 %collective-permute-start.2 = (f32[8,128]{1,0:T(8,128)}, f32[8,128]{1,0:T(8,128)S(1)}, u32[]{:S(2)}, u32[]{:S(2)}) collective-permute-start(f32[8,128]{1,0:T(8,128)} %square_kernel.1.refs_1_), channel_id=1, source_target_pairs={{0,1},{1,2},{2,3},{3,0},{4,5},{5,6},{6,7},{7,4},{8,9},{9,10},{10,1... | collective-permute-start | bytes 12296 | tf_op jit(solution)/shard_map/ppermute | solution.py:262
  79.2 4.5 %copy-start.2 = (f32[8,128]{1,0:T(8,128)}, f32[8,128]{1,0:T(8,128)S(1)}, u32[]{:S(2)}) copy-start(f32[8,128]{1,0:T(8,128)S(1)} %collective-permute-done.4.refs_4_) | copy-start | bytes 12292
  81.8 1.8 %copy-start.3 = (f32[8,128]{1,0:T(8,128)}, f32[8,128]{1,0:T(8,128)S(1)}, u32[]{:S(2)}) copy-start(f32[8,128]{1,0:T(8,128)S(1)} %collective-permute-done.3.refs_3_) | copy-start | bytes 12292
  83.7 0.6 copy-start.4
